TPU v7x, 256 devices: a whole 4x4x8 slice. The times are simulated.
256 devices in a mesh: ctx: 32 (over y, z), head: 8 (over x, core).
Axes of the slice: x: 4, y: 4, z: 8, core: 2. Of those that a mesh axis runs over, the one named last changes fastest.
Arguments:
- queries: bfloat16 [8192, 4096], P('ctx', 'head'), may hold values from -6 to 6
- key_rows: bfloat16 [8192, 4096], P('ctx', 'head'), may hold values from -0.5 to 0.5
- value_rows: bfloat16 [8192, 4096], P('ctx', 'head'), may hold values from -6 to 6
- doc_ids: int32 [8192], P('ctx'), may hold values from 0 to 15, never falling along the last dimension, each value on 1 to 2048 neighbouring positions
- out_grad: bfloat16 [8192, 6144], P(('ctx', 'head')), may hold values from -6 to 6
- out_weight: bfloat16 [4096, 6144], P('head', 'ctx'), may hold values from -0.09375 to 0.09375
Outputs:
- layer_out: bfloat16 [8192, 6144], P(('ctx', 'head'))
- query_grad: bfloat16 [8192, 4096], P('ctx', 'head')
- key_grad: bfloat16 [8192, 4096], P('ctx', 'head')
- value_grad: bfloat16 [8192, 4096], P('ctx', 'head')
- weight_grad: bfloat16 [4096, 6144], P(('head', 'ctx'))
Inputs may be any that keep to these rules, and one draw needn't show every extreme that they name: `doc_ids`: repository ids never fall along the sequence; each repository covers 1 to 2048 tokens, and one covers exactly that many.
All inputs are finite; a program needn't handle non-finite values.
Results may differ from a plain program's by a relative error of at most 0.025.
Values may be sent and summed in bfloat16 or wider, within the bound.
No kernel may reach another device: no remote copies, remote signals or barrier semaphores. Data moves between devices by JAX's collectives and lax.ppermute only.
A program may use at most 128 MiB of HBM per device.

v0:
```python
import jax
import jax.numpy as jnp
from jax import lax
from jax.sharding import PartitionSpec as P

HD = 128
EPSILON = 1e-05


def carried_in(x, axis, join, neutral, backward):
    count = lax.axis_size(axis)
    place = lax.axis_index(axis)
    ahead = count - 1 - place if backward else place
    gathered = jax.tree.map(
        lambda a, kind: lax.all_gather(a.astype(kind), axis),
        x,
        (jnp.bfloat16, jnp.bfloat16, jnp.bfloat16),
    )
    state = jax.tree.map(lambda a, e: jnp.zeros_like(a) + jnp.asarray(e, a.dtype), x, neutral)

    def one(lap, state):
        source = count - 1 - lap if backward else lap
        return join(
            state,
            jax.tree.map(
                lambda a, own: lax.dynamic_index_in_dim(a, source, 0, False).astype(own.dtype),
                gathered,
                x,
            ),
        )

    return lax.fori_loop(0, ahead, one, state)


def forward_link(earlier_part, later_part):
    early_first, early_last, early_state = earlier_part
    late_first, late_last, late_state = later_part
    late_empty = late_last < 0.0
    early_empty = early_last < 0.0
    linked = (early_last == late_first) & (late_first == late_last)
    joined = late_state + jnp.where(linked, early_state, jnp.float32(0.0))
    return (
        jnp.where(early_empty, late_first, early_first),
        jnp.where(late_empty, early_last, late_last),
        jnp.where(late_empty, early_state, joined),
    )


def backward_link(earlier_part, later_part):
    high_first, high_last, high_state = earlier_part
    low_first, low_last, low_state = later_part
    low_empty = low_last < 0.0
    high_empty = high_last < 0.0
    linked = (high_first == low_last) & (low_first == low_last)
    joined = low_state + jnp.where(linked, high_state, jnp.float32(0.0))
    return (
        jnp.where(low_empty, high_first, low_first),
        jnp.where(high_empty, low_last, high_last),
        jnp.where(low_empty, high_state, joined),
    )


def shards(queries, key_rows, value_rows, doc_ids, out_grad, out_weight):
    tok_count, full_width = queries.shape
    head_count = full_width // HD
    query_heads = queries.reshape(tok_count, head_count, HD)
    key_heads = key_rows.reshape(tok_count, head_count, HD)
    value_heads = value_rows.reshape(tok_count, head_count, HD)
    doc_values = doc_ids.astype(jnp.float32)
    first_doc = doc_values[:1]
    last_doc = doc_values[-1:]
    causal = jnp.tril(jnp.ones((tok_count, tok_count), dtype=bool))
    allowed = (causal & (doc_ids[:, None] == doc_ids[None, :]))[None]
    scores = jnp.einsum("thd,shd->hts", query_heads, key_heads, preferred_element_type=jnp.float32)
    weights = jnp.where(allowed, scores, jnp.float32(0.0)).astype(jnp.bfloat16)
    key_last = jnp.where(
        (doc_values == last_doc)[:, None, None], key_heads, jnp.zeros_like(key_heads)
    )
    local_state = jnp.einsum(
        "thd,the->hde", key_last, value_heads, preferred_element_type=jnp.float32
    )
    empty_marks = jnp.full((1,), -1.0, jnp.float32)
    identity = (empty_marks, empty_marks, jnp.zeros_like(local_state))
    prior_first, prior_last, prior_state = carried_in(
        (first_doc, last_doc, local_state), "ctx", forward_link, identity, False
    )
    row_mask = doc_values == prior_last
    prior_rounded = prior_state.astype(jnp.bfloat16)
    inter = jnp.einsum(
        "thd,hde->the", query_heads, prior_rounded, preferred_element_type=jnp.float32
    )
    mixed = jnp.einsum(
        "hts,she->the", weights, value_heads, preferred_element_type=jnp.float32
    ) + jnp.where(row_mask[:, None, None], inter, jnp.float32(0.0))
    inv_norm = lax.rsqrt(jnp.mean(mixed * mixed, axis=-1, keepdims=True) + EPSILON)
    normed = mixed * inv_norm
    normed_flat = normed.astype(jnp.bfloat16).reshape(tok_count, full_width)
    full_weight = lax.all_gather(out_weight, "ctx", axis=1, tiled=True)
    layer_out = lax.psum_scatter(
        jnp.dot(normed_flat, full_weight, preferred_element_type=jnp.float32).astype(jnp.bfloat16),
        "head",
        scatter_dimension=0,
        tiled=True,
    )
    grad_full = lax.all_gather(out_grad, "head", axis=0, tiled=True)
    grad_normed = lax.dot_general(
        grad_full, full_weight, (((1,), (1,)), ((), ())), preferred_element_type=jnp.float32
    ).reshape(tok_count, head_count, HD)
    mixed_grad = (
        inv_norm * (grad_normed - normed * jnp.mean(grad_normed * normed, axis=-1, keepdims=True))
    ).astype(jnp.bfloat16)
    weight_grad = lax.psum_scatter(
        lax.dot_general(
            normed_flat, grad_full, (((0,), (0,)), ((), ())), preferred_element_type=jnp.float32
        ).astype(jnp.bfloat16),
        "ctx",
        scatter_dimension=0,
        tiled=True,
    )
    query_first = jnp.where(
        (doc_values == first_doc)[:, None, None], query_heads, jnp.zeros_like(query_heads)
    )
    local_future = jnp.einsum(
        "thd,the->hde", query_first, mixed_grad, preferred_element_type=jnp.float32
    )
    later_first, later_last, future_state = carried_in(
        (first_doc, last_doc, local_future), "ctx", backward_link, identity, True
    )
    col_mask = (doc_values == later_first)[:, None, None]
    future_rounded = future_state.astype(jnp.bfloat16)
    grad_raw = jnp.einsum(
        "the,she->hts", mixed_grad, value_heads, preferred_element_type=jnp.float32
    )
    grad_scores = jnp.where(allowed, grad_raw, jnp.float32(0.0)).astype(jnp.bfloat16)
    query_grad = jnp.einsum(
        "hts,shd->thd", grad_scores, key_heads, preferred_element_type=jnp.float32
    ) + jnp.where(
        row_mask[:, None, None],
        jnp.einsum("the,hde->thd", mixed_grad, prior_rounded, preferred_element_type=jnp.float32),
        jnp.float32(0.0),
    )
    key_grad = jnp.einsum(
        "hts,thd->shd", grad_scores, query_heads, preferred_element_type=jnp.float32
    ) + jnp.where(
        col_mask,
        jnp.einsum("she,hde->shd", value_heads, future_rounded, preferred_element_type=jnp.float32),
        jnp.float32(0.0),
    )
    value_grad = jnp.einsum(
        "hts,the->she", weights, mixed_grad, preferred_element_type=jnp.float32
    ) + jnp.where(
        col_mask,
        jnp.einsum("shd,hde->she", key_heads, future_rounded, preferred_element_type=jnp.float32),
        jnp.float32(0.0),
    )
    return (
        layer_out,
        query_grad.astype(jnp.bfloat16).reshape(tok_count, full_width),
        key_grad.astype(jnp.bfloat16).reshape(tok_count, full_width),
        value_grad.astype(jnp.bfloat16).reshape(tok_count, full_width),
        weight_grad,
    )


def solution(mesh):
    return jax.shard_map(
        shards,
        mesh=mesh,
        in_specs=(
            P("ctx", "head"),
            P("ctx", "head"),
            P("ctx", "head"),
            P("ctx"),
            P(("ctx", "head"), None),
            P("head", "ctx"),
        ),
        out_specs=(
            P(("ctx", "head"), None),
            P("ctx", "head"),
            P("ctx", "head"),
            P("ctx", "head"),
            P(("head", "ctx"), None),
        ),
        check_vma=False,
    )
```

profile of v0, /device:TPU:2, one launch (start us, length us, event | category | flops | bytes accessed | tf_op | source)
XLA Modules:
  0.0 609.2 jit_solution(14436302235198908007)
XLA Ops:
  7.9 1.1 copy.86
  9.6 2.0 broadcast_compare_fusion.1
  14.0 1.3 dynamic-slice
  15.9 1.4 dynamic-update-slice
  17.3 1.4 dynamic-update-slice.1
  18.7 78.3 %all-reduce.2 = (bf16[32]{0:T(256)(128)(2,1)S(1)}, bf16[32]{0:T(256)(128)(2,1)S(1)}) all-reduce(bf16[32]{0:T(256)(128)(2,1)S(1)} %dynamic-update-slice, bf16[32]{0:T(256)(128)(2,1)S(1)} %dynamic-update-slice.1), channel_id=2, replica_groups=mesh['ctx'=32,'head'=8] {'ctx'}, use_global_device_ids=true, to_apply=%add | all-reduce | flops 64 | bytes 256
  97.0 1.1 copy.59
  99.0 1.3 fusion.2
  101.0 24.8 %all-gather.11.cloned.1.call-done = bf16[256,6144]{1,0:T(8,128)(2,1)} async-done(((bf16[32,6144]{1,0:T(8,128)(2,1)}), bf16[256,6144]{1,0:T(8,128)(2,1)}) %all-gather.11.cloned.1.call-update) | async-done | bytes 3145744 | tf_op jit(solution)/shard_map/all_gather | solution.py:105
  125.8 92.5 %all-gather.9.cloned.1.call-done = bf16[512,6144]{0,1:T(8,128)(2,1)} async-done(((bf16[512,192]{0,1:T(8,128)(2,1)}), bf16[512,6144]{0,1:T(8,128)(2,1)}) %all-gather.9.cloned.1.call-update) | async-done | bytes 6291472 | tf_op jit(solution)/shard_map/all_gather | solution.py:98
  218.2 6.3 %multiply_reduce_fusion = (f32[256,4]{0,1:T(4,128)S(1)}, f32[256,512]{0,1:T(8,128)S(1)}) fusion(f32[256,4,128]{0,2,1:T(8,128)S(1)} %get-tuple-element.234, f32[256,4]{0,1:T(4,128)S(1)} %add_rsqrt_fusion, bf16[256,6144]{1,0:T(8,128)(2,1)} %all-gather.11.cloned.1.call-done, bf16[512,6144]{0,1:T(8,128)(2,1)} %all-gather.9.cloned.1.call-done), kind=kOutput, calls=%fused_computation.34 | convolution fusion | flops 1611004928 | bytes 10493952 | tf_op jit(solution)/shard_map/dot_general | solution.py:106
  224.7 0.9 convolution_convert_fusion.2
  225.6 6.4 %convolution_convert_fusion.1 = bf16[256,6144]{1,0:T(8,128)(2,1)} fusion(bf16[256,512]{0,1:T(8,128)(2,1)S(1)} %bitcast.132, bf16[512,6144]{0,1:T(8,128)(2,1)} %all-gather.9.cloned.1.call-done), kind=kOutput, calls=%fused_computation.9 | convolution fusion | flops 1612185600 | bytes 9699328 | tf_op jit(solution)/shard_map/dot_general | solution.py:100
  232.1 6.4 %convolution_convert_fusion = bf16[512,6144]{1,0:T(8,128)(2,1)} fusion(bf16[256,512]{0,1:T(8,128)(2,1)S(1)} %bitcast.133, bf16[256,6144]{1,0:T(8,128)(2,1)} %all-gather.11.cloned.1.call-done), kind=kOutput, calls=%fused_computation.8 | convolution fusion | flops 1613758464 | bytes 9699328 | tf_op jit(solution)/shard_map/dot_general | solution.py:113
  240.7 94.9 %all-gather.15.cloned.1.call-done = bf16[128,128,128]{2,1,0:T(8,128)(2,1)} async-done(((bf16[4,128,128]{2,1,0:T(8,128)(2,1)}), bf16[128,128,128]{2,1,0:T(8,128)(2,1)}) %all-gather.15.cloned.1.call-update) | async-done | bytes 4194320 | tf_op jit(solution)/shard_map/all_gather | solution.py:15
  335.7 158.6 %while.31 = (s32[]{:T(128)}, f32[1]{0:T(128)}, f32[4,128,128]{2,1,0:T(8,128)S(1)}, s32[]{:T(128)}, bf16[32,1]{0,1:T(2,128)(2,1)S(1)}, /*index=5*/bf16[32,1]{0,1:...) while((s32[]{:T(128)}, f32[1]{0:T(128)}, ...), condition=%wide.region_6.7_spmd, body=%wide.region_5.6_spmd.sunk | while | flops 262155 | bytes 655590 | solution.py:32
  339.7 1.0 fusion.69
  344.8 1.0 fusion.69
  350.0 1.0 fusion.69
  355.1 1.0 fusion.69
  360.2 1.0 fusion.69
  365.3 1.0 fusion.69
  370.4 1.0 fusion.69
  375.5 1.0 fusion.69
  380.7 1.0 fusion.69
  385.8 1.0 fusion.69
  390.9 1.0 fusion.69
  396.0 1.0 fusion.69
  401.1 1.0 fusion.69
  406.2 1.0 fusion.69
  411.3 1.0 fusion.69
  416.5 1.0 fusion.69
  421.6 1.0 fusion.69
  426.7 1.0 fusion.69
  431.8 1.0 fusion.69
  436.9 1.0 fusion.69
  442.0 1.1 fusion.69
  447.2 1.0 fusion.69
  452.3 1.0 fusion.69
  457.4 1.0 fusion.69
  462.5 1.0 fusion.69
  467.6 1.0 fusion.69
  472.7 1.0 fusion.69
  477.9 1.0 fusion.69
  483.0 1.0 fusion.69
  488.1 1.0 fusion.69
  493.2 1.0 fusion.69
  496.5 105.9 %reduce-scatter.5.cloned.1.call-done = bf16[16,6144]{1,0:T(8,128)(2,1)} async-done(((bf16[512,6144]{1,0:T(8,128)(2,1)}), bf16[16,6144]{1,0:T(8,128)(2,1)}) %reduce-scatter.5.cloned.1.call-update) | async-done | bytes 196624 | tf_op jit(solution)/shard_map/reduce_scatter | solution.py:112
  (78 shorter events, 31.2 us)
Async XLA Ops:
  7.2 4.4 copy-start
  7.2 93.4 %all-gather.13.cloned.1.call-start = ((), (), s32[]{:S(2)}) async-start(), calls=%async_computation.6 | async-start | bytes 4325376 | tf_op jit(solution)/shard_map/all_gather | solution.py:15
  11.6 89.1 %copy-start.2 = (s32[256]{0:T(256)S(1)}, s32[256]{0:T(256)}, u32[]{:S(2)}) copy-start(s32[256]{0:T(256)} %param.13) | copy-start | bytes 3076
  12.5 113.3 %all-gather.11.cloned.1.call-start = ((), (), s32[]{:S(2)}) async-start(), calls=%async_computation.4 | async-start | bytes 3538944 | tf_op jit(solution)/shard_map/all_gather | solution.py:105
  13.2 205.0 %all-gather.9.cloned.1.call-start = ((), (), s32[]{:S(2)}) async-start(), calls=%async_computation.2 | async-start | bytes 6488064 | tf_op jit(solution)/shard_map/all_gather | solution.py:98
  14.0 321.7 %all-gather.15.cloned.1.call-start = ((), (), s32[]{:S(2)}) async-start(), calls=%async_computation.7 | async-start | bytes 4325376 | tf_op jit(solution)/shard_map/all_gather | solution.py:15
  225.6 270.9 %reduce-scatter.3.cloned.1.call-start = ((), (), s32[]{:S(2)}) async-start(), calls=%async_computation.3 | async-start | bytes 3538944 | tf_op jit(solution)/shard_map/reduce_scatter | solution.py:99
  232.1 370.3 %reduce-scatter.5.cloned.1.call-start = ((), (), s32[]{:S(2)}) async-start(), calls=%async_computation.5 | async-start | bytes 6488064 | tf_op jit(solution)/shard_map/reduce_scatter | solution.py:112
  240.2 255.1 %copy-start.1 = (bf16[256,512]{1,0:T(8,128)(2,1)S(1)}, bf16[256,512]{1,0:T(8,128)(2,1)}, u32[]{:S(2)}) copy-start(bf16[256,512]{1,0:T(8,128)(2,1)} %param.11) | copy-start | bytes 786436
Sparse Core Ops, SparseCore 0:
  12.6 84.7 all-gather.12
  99.3 26.4 all-gather.10
  128.3 89.8 all-gather.8
  225.7 109.8 all-gather.14
  338.6 32.1 reduce-scatter.2
  375.2 227.1 reduce-scatter.4
where the time goes:
time: 612 us; the launch traced here: 609 us
  waiting for transfers between devices  320 us (52%)
  loops' own time  105 us (17%)
  blocking collectives  78.3 us (13%)
  other arithmetic  36.1 us (6%)
  local copies, waits for them, and re-layouts  30.8 us (5%)
  matrix products  24.5 us (4%)
  between operations  14.3 us (2%)
    reduce_scatter x1, waiting for transfers between devices, shards(): lax.psum_scatter(lax.dot_general(normed_flat, grad_full, (((0,), (0,)), (...  106 us
    another operation x2, loops' own time, carried_in(): return lax.fori_loop(0, ahead, one, state)  105 us
    all_gather x2, waiting for transfers between devices, carried_in(): lax.all_gather(a.astype(kind), axis)  95 us
    all_gather x1, waiting for transfers between devices, shards(): full_weight = lax.all_gather(out_weight, 'ctx', axis=1, tiled=True)  92.5 us
    unnamed x1, blocking collectives  78.3 us
    select_n x31, other arithmetic, backward_link(): jnp.where(low_empty, high_state, joined)  32.4 us
    all_gather x1, waiting for transfers between devices, shards(): grad_full = lax.all_gather(out_grad, 'head', axis=0, tiled=True)  24.8 us
    dynamic_slice x31, local copies, waits for them, and re-layouts, one(): lax.dynamic_index_in_dim(a, source, 0, False).astype(own.dtype)  20.8 us
  transfers between devices with their start and end apart: 6, of which 4 were waited for; matrix products, arithmetic and copies ran while one was open for 13% of the time, Pallas kernels for 0%

commit v1 on v0

--- a/solution.py
+++ b/solution.py
@@ -5,6 +5,22 @@
 
 HD = 128
 EPSILON = 1e-05
+
+
+def ring_gather(x, axis, dim):
+    ways, here, step = (lax.axis_size(axis), lax.axis_index(axis), x.shape[dim])
+    shape = [n * ways if d == dim else n for d, n in enumerate(x.shape)]
+    full = lax.dynamic_update_slice_in_dim(jnp.zeros(shape, x.dtype), x, here * step, axis=dim)
+    going_up = going_down = x
+    for far in range(1, ways // 2 + 1):
+        going_up = lax.ppermute(going_up, axis, [(d, (d + 1) % ways) for d in range(ways)])
+        full = lax.dynamic_update_slice_in_dim(full, going_up, (here - far) % ways * step, axis=dim)
+        if 2 * far < ways:
+            going_down = lax.ppermute(going_down, axis, [(d, (d - 1) % ways) for d in range(ways)])
+            full = lax.dynamic_update_slice_in_dim(
+                full, going_down, (here + far) % ways * step, axis=dim
+            )
+    return full
 
 
 def carried_in(x, axis, join, neutral, backward):
@@ -102,7 +118,7 @@
         scatter_dimension=0,
         tiled=True,
     )
-    grad_full = lax.all_gather(out_grad, "head", axis=0, tiled=True)
+    grad_full = ring_gather(out_grad, "head", 0)
     grad_normed = lax.dot_general(
         grad_full, full_weight, (((1,), (1,)), ((), ())), preferred_element_type=jnp.float32
     ).reshape(tok_count, head_count, HD)

time: 612 us -> 662 us (1.082)
  waiting for transfers between devices: 320 us -> 363 us
    all_gather x2, waiting for transfers between devices: 95 us -> 177 us  [carried_in(): lax.all_gather(a.astype(kind), axis)]
    all_gather x1, waiting for transfers between devices: 92.5 us -> 57.6 us  [shards(): full_weight = lax.all_gather(out_weight, 'ctx', axis=1, tiled=True)]
    all_gather x1 -> x0, waiting for transfers between devices: 24.8 us -> none  [shards(): grad_full = lax.all_gather(out_grad, 'head', axis=0, tiled=True)]
    ppermute x0 -> x7, waiting for transfers between devices: none -> 15.8 us  [the longest x4 15.7 us: ring_gather(): lax.ppermute(going_up, axis, [(d, (d + 1) % ways) for d in range(ways)])]
  transfers between devices with their start and end apart: 6 -> 12, of which waited for: 4 -> 7; matrix products, arithmetic and copies ran while one was open for 13% -> 12% of each run, Pallas kernels for 0% -> 0%
where the time goes in v1:
time: 662 us; the launch traced here: 660 us
  waiting for transfers between devices  363 us (55%)
  loops' own time  102 us (15%)
  blocking collectives  78.3 us (12%)
  other arithmetic  36.8 us (6%)
  local copies, waits for them, and re-layouts  34 us (5%)
  matrix products  25.6 us (4%)
  between operations  14.2 us (2%)
    all_gather x2, waiting for transfers between devices, carried_in(): lax.all_gather(a.astype(kind), axis)  177 us
    reduce_scatter x1, waiting for transfers between devices, shards(): lax.psum_scatter(lax.dot_general(normed_flat, grad_full, (((0,), (0,)), (...  112 us
    another operation x2, loops' own time, carried_in(): return lax.fori_loop(0, ahead, one, state)  102 us
    unnamed x1, blocking collectives  78.3 us
    all_gather x1, waiting for transfers between devices, shards(): full_weight = lax.all_gather(out_weight, 'ctx', axis=1, tiled=True)  57.6 us
    select_n x31, other arithmetic, backward_link(): jnp.where(low_empty, high_state, joined)  32.4 us
    dynamic_slice x31, local copies, waits for them, and re-layouts, one(): lax.dynamic_index_in_dim(a, source, 0, False).astype(own.dtype)  18.4 us
    ppermute x4, waiting for transfers between devices, ring_gather(): lax.ppermute(going_up, axis, [(d, (d + 1) % ways) for d in range(ways)])  15.7 us
  transfers between devices with their start and end apart: 12, of which 7 were waited for; matrix products, arithmetic and copies ran while one was open for 12% of the time, Pallas kernels for 0%

profile of v1, /device:TPU:2, one launch (start us, length us, event | category | flops | bytes accessed | tf_op | source)
XLA Modules:
  0.0 659.7 jit_solution(11807138588603772672)
XLA Ops:
  7.9 1.1 copy.86
  9.6 2.0 broadcast_compare_fusion.1
  13.3 1.3 dynamic-slice
  15.2 1.4 dynamic-update-slice
  16.6 1.4 dynamic-update-slice.1
  18.0 1.7 collective-permute-start.1
  19.7 78.3 %all-reduce.2 = (bf16[32]{0:T(256)(128)(2,1)S(1)}, bf16[32]{0:T(256)(128)(2,1)S(1)}) all-reduce(bf16[32]{0:T(256)(128)(2,1)S(1)} %dynamic-update-slice, bf16[32]{0:T(256)(128)(2,1)S(1)} %dynamic-update-slice.1), channel_id=2, replica_groups=mesh['ctx'=32,'head'=8] {'ctx'}, use_global_device_ids=true, to_apply=%add | all-reduce | flops 64 | bytes 256
  98.1 1.8 copy.59
  101.2 1.3 fusion.2
  102.5 1.1 convolution_bitcast_fusion.2
  103.7 1.7 collective-permute-start.3
  107.5 3.6 collective-permute-done.2
  111.1 2.0 collective-permute-start.5
  113.2 5.1 collective-permute-done.4
  118.4 7.0 %collective-permute-done.6 = bf16[32,6144]{1,0:T(8,128)(2,1)S(1)} collective-permute-done((bf16[32,6144]{1,0:T(8,128)(2,1)S(1)}, bf16[32,6144]{1,0:T(8,128)(2,1)S(1)}, u32[]{:S(2)}, u32[]{:S(2)}) %collective-permute-start.6) | collective-permute-done | bytes 393248 | tf_op jit(solution)/shard_map/ppermute | solution.py:16
  126.3 2.3 multiply_reduce_fusion.1
  128.6 57.6 %all-gather.8.cloned.1.call-done = bf16[512,6144]{0,1:T(8,128)(2,1)} async-done(((bf16[512,192]{0,1:T(8,128)(2,1)}), bf16[512,6144]{0,1:T(8,128)(2,1)}) %all-gather.8.cloned.1.call-update) | async-done | bytes 6291472 | tf_op jit(solution)/shard_map/all_gather | solution.py:114
  186.1 5.5 multiply_reduce_fusion
  194.1 6.5 convolution_convert_fusion.1
  200.7 5.4 convolution_convert_fusion
  209.3 177.0 %all-gather.12.cloned.1.call-done = bf16[128,128,128]{2,1,0:T(8,128)(2,1)} async-done(((bf16[4,128,128]{2,1,0:T(8,128)(2,1)}), bf16[128,128,128]{2,1,0:T(8,128)(2,1)}) %all-gather.12.cloned.1.call-update) | async-done | bytes 4194320 | tf_op jit(solution)/shard_map/all_gather | solution.py:31
  386.3 152.5 %while.31 = (s32[]{:T(128)}, f32[1]{0:T(128)}, f32[4,128,128]{2,1,0:T(8,128)S(1)}, s32[]{:T(128)}, bf16[32,1]{0,1:T(2,128)(2,1)S(1)}, /*index=5*/bf16[32,1]{0,1:...) while((s32[]{:T(128)}, f32[1]{0:T(128)}, ...), condition=%wide.region_6.7_spmd, body=%wide.region_5.6_spmd.sunk | while | flops 262155 | bytes 655590 | solution.py:48
  390.2 1.0 fusion.69
  395.1 1.0 fusion.69
  400.0 1.0 fusion.69
  405.0 1.0 fusion.69
  409.9 1.0 fusion.69
  414.8 1.0 fusion.69
  419.7 1.0 fusion.69
  424.6 1.0 fusion.69
  439.4 1.1 fusion.69
  454.2 1.0 fusion.69
  459.1 1.0 fusion.69
  464.0 1.0 fusion.69
  468.9 1.0 fusion.69
  473.8 1.0 fusion.69
  483.7 1.0 fusion.69
  488.6 1.0 fusion.69
  493.5 1.0 fusion.69
  498.4 1.0 fusion.69
  503.3 1.0 fusion.69
  508.2 1.0 fusion.69
  513.2 1.0 fusion.69
  518.1 1.0 fusion.69
  523.0 1.0 fusion.69
  527.9 1.0 fusion.69
  532.8 1.0 fusion.69
  541.0 112.1 %reduce-scatter.5.cloned.1.call-done = bf16[16,6144]{1,0:T(8,128)(2,1)} async-done(((bf16[512,6144]{1,0:T(8,128)(2,1)}), bf16[16,6144]{1,0:T(8,128)(2,1)}) %reduce-scatter.5.cloned.1.call-update) | async-done | bytes 196624 | tf_op jit(solution)/shard_map/reduce_scatter | solution.py:128
  (122 shorter events, 40.4 us)
Async XLA Ops:
  7.2 4.4 copy-start
  7.2 118.3 %all-gather.10.cloned.1.call-start = ((), (), s32[]{:S(2)}) async-start(), calls=%async_computation.5 | async-start | bytes 4325376 | tf_op jit(solution)/shard_map/all_gather | solution.py:31
  9.0 90.9 %copy-start.11 = (bf16[256,512]{0,1:T(8,128)(2,1)}, bf16[256,512]{0,1:T(8,128)(2,1)S(1)}, u32[]{:S(2)}) copy-start(bf16[256,512]{0,1:T(8,128)(2,1)S(1)} %copy.86) | copy-start | bytes 786436
  12.5 173.6 %all-gather.8.cloned.1.call-start = ((), (), s32[]{:S(2)}) async-start(), calls=%async_computation.2 | async-start | bytes 6488064 | tf_op jit(solution)/shard_map/all_gather | solution.py:114
  13.3 373.1 %all-gather.12.cloned.1.call-start = ((), (), s32[]{:S(2)}) async-start(), calls=%async_computation.6 | async-start | bytes 4325376 | tf_op jit(solution)/shard_map/all_gather | solution.py:31
  13.3 90.3 %collective-permute-start = (bf16[32,6144]{1,0:T(8,128)(2,1)}, bf16[32,6144]{1,0:T(8,128)(2,1)}, u32[]{:S(2)}, u32[]{:S(2)}) collective-permute-start(bf16[32,6144]{1,0:T(8,128)(2,1)} %param.14), channel_id=1, source_target_pairs={{0,1},{1,2},{2,3},{3,4},{4,5},{5,6},{6,7},{7,0},{8,9},{9,10},{10,1... | collective-permute-start | bytes 1179656 | tf_op jit(solution)/shard_map/ppermute | solution.py:16
  18.0 85.6 %collective-permute-start.1 = (bf16[32,6144]{1,0:T(8,128)(2,1)}, bf16[32,6144]{1,0:T(8,128)(2,1)}, u32[]{:S(2)}, u32[]{:S(2)}) collective-permute-start(bf16[32,6144]{1,0:T(8,128)(2,1)} %param.14), channel_id=1, source_target_pairs={{0,7},{1,0},{2,1},{3,2},{4,3},{5,4},{6,5},{7,6},{8,15},{9,8},{10,9... | collective-permute-start | bytes 1179656 | tf_op jit(solution)/shard_map/ppermute | solution.py:19
  99.9 1.2 copy-start.13
  99.9 1.3 copy-start.5
  102.5 15.9 %copy-start.8 = (bf16[4,256,256]{2,1,0:T(8,128)(2,1)}, bf16[4,256,256]{2,1,0:T(8,128)(2,1)S(1)}, u32[]{:S(2)}) copy-start(bf16[4,256,256]{2,1,0:T(8,128)(2,1)S(1)} %fusion.2) | copy-start | bytes 1572868
  103.6 7.4 %collective-permute-start.2 = (bf16[32,6144]{1,0:T(8,128)(2,1)}, bf16[32,6144]{1,0:T(8,128)(2,1)S(1)}, u32[]{:S(2)}, u32[]{:S(2)}) collective-permute-start(bf16[32,6144]{1,0:T(8,128)(2,1)} %collective-permute-done), channel_id=1, source_target_pairs={{0,1},{1,2},{2,3},{3,4},{4,5},{5,6},{6,7},{7,0},{8,9},{9,10},{10,1... | collective-permute-start | bytes 1179656 | tf_op jit(solution)/shard_map/ppermute | solution.py:16
  103.7 7.4 %collective-permute-start.3 = (bf16[32,6144]{1,0:T(8,128)(2,1)}, bf16[32,6144]{1,0:T(8,128)(2,1)S(1)}, u32[]{:S(2)}, u32[]{:S(2)}) collective-permute-start(bf16[32,6144]{1,0:T(8,128)(2,1)} %collective-permute-done.1), channel_id=1, source_target_pairs={{0,7},{1,0},{2,1},{3,2},{4,3},{5,4},{6,5},{7,6},{8,15},{9,8},{10,9... | collective-permute-start | bytes 1179656 | tf_op jit(solution)/shard_map/ppermute | solution.py:19
  111.1 7.2 %collective-permute-start.4 = (bf16[32,6144]{1,0:T(8,128)(2,1)S(1)}, bf16[32,6144]{1,0:T(8,128)(2,1)S(1)}, u32[]{:S(2)}, u32[]{:S(2)}) collective-permute-start(bf16[32,6144]{1,0:T(8,128)(2,1)S(1)} %collective-permute-done.2), channel_id=1, source_target_pairs={{0,1},{1,2},{2,3},{3,4},{4,5},{5,6},{6,7},{7,0},{8,9},{9,10},{10,1... | collective-permute-start | bytes 1179656 | tf_op jit(solution)/shard_map/ppermute | solution.py:16
  111.1 7.3 %collective-permute-start.5 = (bf16[32,6144]{1,0:T(8,128)(2,1)S(1)}, bf16[32,6144]{1,0:T(8,128)(2,1)S(1)}, u32[]{:S(2)}, u32[]{:S(2)}) collective-permute-start(bf16[32,6144]{1,0:T(8,128)(2,1)S(1)} %collective-permute-done.3), channel_id=1, source_target_pairs={{0,7},{1,0},{2,1},{3,2},{4,3},{5,4},{6,5},{7,6},{8,15},{9,8},{10,9... | collective-permute-start | bytes 1179656 | tf_op jit(solution)/shard_map/ppermute | solution.py:19
  113.2 13.1 %copy-start.14 = (s32[256]{0:T(256)S(1)}, s32[256]{0:T(256)}, u32[]{:S(2)}) copy-start(s32[256]{0:T(256)} %param.13) | copy-start | bytes 3076
  118.3 7.2 %collective-permute-start.6 = (bf16[32,6144]{1,0:T(8,128)(2,1)S(1)}, bf16[32,6144]{1,0:T(8,128)(2,1)S(1)}, u32[]{:S(2)}, u32[]{:S(2)}) collective-permute-start(bf16[32,6144]{1,0:T(8,128)(2,1)S(1)} %collective-permute-done.4), channel_id=1, source_target_pairs={{0,1},{1,2},{2,3},{3,4},{4,5},{5,6},{6,7},{7,0},{8,9},{9,10},{10,1... | collective-permute-start | bytes 1179656 | tf_op jit(solution)/shard_map/ppermute | solution.py:16
  186.1 5.5 copy-start.2
  186.1 7.0 %copy-start.6 = (bf16[256,512]{0,1:T(8,128)(2,1)S(1)}, bf16[256,512]{0,1:T(8,128)(2,1)}, u32[]{:S(2)}) copy-start(bf16[256,512]{0,1:T(8,128)(2,1)} %copy.59) | copy-start | bytes 786436
  192.4 0.7 copy-start.3
  194.1 347.0 %reduce-scatter.3.cloned.1.call-start = ((), (), s32[]{:S(2)}) async-start(), calls=%async_computation.3 | async-start | bytes 3538944 | tf_op jit(solution)/shard_map/reduce_scatter | solution.py:115
  200.6 452.5 %reduce-scatter.5.cloned.1.call-start = ((), (), s32[]{:S(2)}) async-start(), calls=%async_computation.4 | async-start | bytes 6488064 | tf_op jit(solution)/shard_map/reduce_scatter | solution.py:128
  206.1 0.9 copy-start.4
  206.1 1.3 copy-start.12
  206.1 1.6 copy-start.1
  206.1 2.7 copy-start.7
  206.1 2.9 copy-start.9
  209.3 330.6 %copy-start.10 = (bf16[256,512]{1,0:T(8,128)(2,1)S(1)}, bf16[256,512]{1,0:T(8,128)(2,1)}, u32[]{:S(2)}) copy-start(bf16[256,512]{1,0:T(8,128)(2,1)} %param.11) | copy-start | bytes 786436
Sparse Core Ops, SparseCore 0:
  12.6 84.8 all-gather.9
  100.1 85.9 all-gather.7
  194.2 192.0 all-gather.11
  389.3 32.1 reduce-scatter.2
  425.9 227.2 reduce-scatter.4
